TPU v7x, 128 devices: a whole 4x4x4 slice. The times are simulated.
128 devices in a mesh: grp: 4 (over y), fsdp: 32 (over x, z, core).
Axes of the slice: x: 4, y: 4, z: 4, core: 2. Of those that a mesh axis runs over, the one named last changes fastest.
Arguments:
- hidden: bfloat16 [256, 257, 1024], P(('grp', 'fsdp')), may hold values from -6 to 6
- ln1_gain: float32 [1024], replicated, may hold values from 0.25 to 1.75
- w_qkv: bfloat16 [1024, 3072], P('fsdp'), may hold values from -0.1875 to 0.1875
- w_out: bfloat16 [1024, 1024], P('fsdp'), may hold values from -0.1875 to 0.1875
- ln2_gain: float32 [1024], replicated, may hold values from 0.25 to 1.75
- w_up: bfloat16 [1024, 4096], P('fsdp'), may hold values from -0.1875 to 0.1875
- w_down: bfloat16 [4096, 1024], P('fsdp'), may hold values from -0.09375 to 0.09375
- post_gain: float32 [1024], replicated, may hold values from 0.25 to 1.75
- w_proj: bfloat16 [1024, 256], replicated, may hold values from -0.1875 to 0.1875
- table: float32 [128, 2048, 256], P(('grp', 'fsdp')), may hold values from -6 to 6
- accum: float32 [128, 2048, 256], P(('grp', 'fsdp')), may hold values from 0.1 to 4
- place: int32 [128], replicated, may hold values from 0 to 127, each once
- lookup_table: int32 [16384, 1], P(('grp', 'fsdp')), may hold values from 0 to 127; in each aligned block of 128 rows (0 to 127, 128 to 255, ...) at most 2 rows name the same one
- lookup_row: int32 [16384], P(('grp', 'fsdp')), may hold values from 0 to 2047
Outputs:
- table_new: float32 [128, 2048, 256], P(('grp', 'fsdp'))
- accum_new: float32 [128, 2048, 256], P(('grp', 'fsdp'))
- content_grad: float32 [256, 256], P(('grp', 'fsdp'))
- proj_grad: float32 [1024, 256], P(('grp', 'fsdp'))
Inputs may be any that keep to these rules, and one draw needn't show every extreme that they name: `lookup_table`: within the lookups of one device (aligned blocks of 128), no table is named more than 2 times, a bound that some block reaches. `place`: every device holds exactly one table.
All inputs are finite; a program needn't handle non-finite values.
Results may differ from a plain program's by a relative error of at most 0.0044.
Values may be sent and summed in bfloat16 or wider, within the bound.
A program may use at most 192 MiB of HBM per device.

v0:
```python
import math
import jax
import jax.numpy as jnp
from jax import lax
from jax.sharding import Mesh
from jax.sharding import PartitionSpec as P

HEADS = 16
LOOK_IMG = 64
FSDP = ("fsdp_0", "fsdp_1", "fsdp_2")
GRP_FSDP = ("grp", "fsdp_0", "fsdp_1", "fsdp_2")
epsilon = 1e-06
learn_rate = 0.5


def sent_together(arrays, axis, dim, along):
    widths = [a.shape[along] for a in arrays]
    both = jnp.concatenate(arrays, axis=along)
    out = lax.all_gather(both, axis, axis=dim, tiled=True)
    return tuple(jnp.split(out, [sum(widths[:k]) for k in range(1, len(widths))], axis=along))


def in_blocks(array, dim, devices):
    shape = array.shape
    tiles = array.reshape(*shape[:dim], devices, shape[dim] // devices, *shape[dim + 1 :])
    return jnp.moveaxis(tiles, dim, 0)


def laid_out(tiles, dim):
    tiles = jnp.moveaxis(tiles, 0, dim)
    shape = tiles.shape
    return tiles.reshape(*shape[:dim], shape[dim] * shape[dim + 1], *shape[dim + 2 :])


def turned_blocks(tiles, axes, sequence):
    shape = [lax.axis_size(a) for a in axes]
    tiles = tiles.reshape(*shape, *tiles.shape[1:])
    for k in sequence:
        tiles = lax.all_to_all(tiles, axes[k], split_axis=k, concat_axis=k, tiled=True)
    return tiles.reshape(-1, *tiles.shape[len(axes) :])


def core_and_chips(array, groups, sequence, split_dim, concat_dim):
    devices = lax.axis_size(groups[0]) * lax.axis_size(groups[1])
    tiles = in_blocks(array, split_dim, devices)
    return laid_out(turned_blocks(tiles, groups, sequence), concat_dim)


def layer_norm(values, gain):
    center = jnp.mean(values, axis=-1, keepdims=True)
    shifted = values - center
    spread = jnp.mean(shifted * shifted, axis=-1, keepdims=True)
    return shifted * lax.rsqrt(spread + epsilon) * gain


def attend(qkv, images, seq, width):
    head_dim = width // HEADS
    parts = qkv.reshape(images, seq, 3, HEADS, head_dim)
    scores = jnp.einsum(
        "bqhd,bkhd->bhqk", parts[:, :, 0], parts[:, :, 1], preferred_element_type=jnp.float32
    ) / math.sqrt(head_dim)
    probs = jax.nn.softmax(scores, axis=-1).astype(jnp.bfloat16)
    mixed = jnp.einsum("bhqk,bkhd->bqhd", probs, parts[:, :, 2], preferred_element_type=jnp.float32)
    return mixed.astype(jnp.bfloat16).reshape(images * seq, width)


def on_device(
    hidden,
    ln1_gain,
    w_qkv,
    w_out,
    ln2_gain,
    w_up,
    w_down,
    post_gain,
    w_proj,
    table,
    accum,
    place,
    lookup_table,
    lookup_row,
):
    images, seq, width = hidden.shape
    count = images * seq
    tokens = hidden.reshape(count, width)
    full_qkv, full_out, full_up, full_down = (
        *sent_together((w_qkv, w_out, w_up), FSDP, 0, 1),
        lax.all_gather(w_down, FSDP, axis=0, tiled=True),
    )
    normed = layer_norm(tokens.astype(jnp.float32), ln1_gain).astype(jnp.bfloat16)
    qkv = jnp.dot(normed, full_qkv, preferred_element_type=jnp.float32)
    mixed = attend(qkv.astype(jnp.bfloat16), images, seq, width)
    projected = jnp.dot(mixed, full_out, preferred_element_type=jnp.float32)
    resid = (tokens.astype(jnp.float32) + projected).astype(jnp.bfloat16)
    normed_two = layer_norm(resid.astype(jnp.float32), ln2_gain).astype(jnp.bfloat16)
    upward = jnp.dot(normed_two, full_up, preferred_element_type=jnp.float32)
    active = jax.nn.gelu(upward, approximate=False).astype(jnp.bfloat16)
    downward = jnp.dot(active, full_down, preferred_element_type=jnp.float32)
    final = resid.astype(jnp.float32) + downward
    posted = layer_norm(final, post_gain).reshape(images, seq, width)
    pooled = jnp.mean(posted, axis=1).astype(jnp.bfloat16)
    content = jnp.dot(pooled, w_proj, preferred_element_type=jnp.float32)
    scale = lax.rsqrt(jnp.mean(content * content, axis=-1, keepdims=True) + epsilon)
    unit = content * scale
    proj_width = unit.shape[1]
    local_table = table[0]
    n_devices = lax.axis_size(GRP_FSDP)
    tables_count = place.shape[0]
    table_ids = jnp.arange(tables_count, dtype=jnp.int32)
    look_dev = lookup_row.shape[0]
    slots = max(2, (2 * look_dev + n_devices - 1) // n_devices)
    owners = jnp.sum(jnp.where(lookup_table == table_ids[None, :], place[None, :], 0), axis=1)
    hits = (owners[:, None] == jnp.arange(n_devices, dtype=jnp.int32)[None, :]).astype(jnp.int32)
    earlier = jnp.cumsum(hits, axis=0) - hits
    position = jnp.sum(earlier * hits, axis=1)
    target = owners * slots + position
    spread_unit = jnp.repeat(unit, LOOK_IMG, axis=0)
    send_vec = jnp.zeros((n_devices * slots, proj_width), jnp.float32).at[target].set(spread_unit)
    send_rows = jnp.full((n_devices * slots,), -1, jnp.int32).at[target].set(lookup_row)
    got_vec, got_rows = (
        core_and_chips(
            send_vec.reshape(n_devices, slots, proj_width),
            (("grp", "fsdp_0", "fsdp_1"), "fsdp_2"),
            (1, 0),
            0,
            0,
        ),
        core_and_chips(
            send_rows.reshape(n_devices, slots),
            (("grp", "fsdp_0", "fsdp_1"), "fsdp_2"),
            (1, 0),
            0,
            0,
        ),
    )
    flat_rows = got_rows.reshape(-1)
    valid = flat_rows >= 0
    safe_rows = jnp.where(valid, flat_rows, 0)
    diff = jnp.where(valid[:, None], local_table[safe_rows] - got_vec.reshape(-1, proj_width), 0.0)
    grad_rows = jnp.zeros(local_table.shape, jnp.float32).at[safe_rows].add(diff)
    returned = lax.all_to_all(
        -diff.reshape(n_devices, slots, proj_width),
        GRP_FSDP,
        split_axis=0,
        concat_axis=0,
        tiled=True,
    )
    per_lookup = returned.reshape(-1, proj_width)[target]
    grad_unit = jnp.sum(per_lookup.reshape(images, LOOK_IMG, proj_width), axis=1)
    accum_new = accum[0] + grad_rows * grad_rows
    table_new = local_table - learn_rate * grad_rows / jnp.sqrt(accum_new)
    inner = jnp.mean(grad_unit * unit, axis=-1, keepdims=True)
    content_grad = scale * (grad_unit - unit * inner)
    share = width // n_devices
    every_grad = lax.all_gather(content_grad, GRP_FSDP, axis=0, tiled=True)
    my_columns = lax.all_to_all(
        pooled.reshape(images, n_devices, share), GRP_FSDP, split_axis=1, concat_axis=0, tiled=True
    )
    column_block = my_columns.reshape(-1, share).astype(jnp.float32)
    proj_grad = jnp.dot(
        column_block.T,
        every_grad,
        precision=lax.Precision.HIGHEST,
        preferred_element_type=jnp.float32,
    )
    return (table_new[None], accum_new[None], content_grad, proj_grad)


def solution(mesh):
    torus = Mesh(
        mesh.devices.reshape(mesh.shape["grp"], 4, 4, 2), ("grp", "fsdp_0", "fsdp_1", "fsdp_2")
    )
    in_specs = (
        P(GRP_FSDP, None, None),
        P(),
        P(FSDP, None),
        P(FSDP, None),
        P(),
        P(FSDP, None),
        P(FSDP, None),
        P(),
        P(),
        P(GRP_FSDP, None, None),
        P(GRP_FSDP, None, None),
        P(),
        P(GRP_FSDP, None),
        P(GRP_FSDP),
    )
    out_specs = (
        P(GRP_FSDP, None, None),
        P(GRP_FSDP, None, None),
        P(GRP_FSDP, None),
        P(GRP_FSDP, None),
    )
    return jax.shard_map(
        on_device, mesh=torus, in_specs=in_specs, out_specs=out_specs, check_vma=False
    )
```

profile of v0, /device:TPU:1, one launch (start us, length us, event | category | flops | bytes accessed | tf_op | source)
XLA Modules:
  0.0 299.2 jit_solution(8550466060743165538)
XLA Ops:
  12.7 4.7 %all_to_all.40 = s32[2,1,128]{2,1,0:T(1,128)S(1)} all-to-all(s32[2,1,128]{2,1,0:T(1,128)S(1)} %reshape.241), channel_id=1, replica_groups=mesh['grp'=4,'fsdp_0'=4,'fsdp_1'=4,'fsdp_2'=2] {'fsdp_2'}, dimensions={0} | all-to-all | bytes 2048 | tf_op jit(solution)/shard_map/all_to_all | solution.py:39
  19.4 11.5 %all-to-all-start.1 = ((s32[64,2,1,2]{3,1,2,0:T(2,128)}), s32[64,2,1,2]{3,1,2,0:T(2,128)S(1)}, u32[]{:S(2)}, u32[]{:S(2)}) async-start(s32[64,2,1,2]{3,1,2,0:T(2,128)} %copy.51), calls=%async_computation.1 | async-start | bytes 131072 | tf_op jit(solution)/shard_map/all_to_all | solution.py:39
  33.1 2.8 multiply_reduce_fusion.2
  40.3 47.6 %all-gather.4.cloned.1.call-done = bf16[1024,8192]{1,0:T(8,128)(2,1)} async-done(((bf16[32,8192]{1,0:T(8,128)(2,1)}), bf16[1024,8192]{1,0:T(8,128)(2,1)}) %all-gather.4.cloned.1.call-update) | async-done | bytes 16777232 | tf_op jit(solution)/shard_map/all_gather | solution.py:19
  87.9 8.8 %fusion.20 = bf16[514,3072]{1,0:T(8,128)(2,1)} fusion(bf16[1024,8192]{1,0:T(8,128)(2,1)} %all-gather.4.cloned.1.call-done, f32[514,1024]{1,0:T(8,128)} %reshape.190, f32[1024]{0:T(1024)S(1)} %copy-done.5, f32[514]{0:T(1024)S(1)} %rsqrt.37, f32[514]{0:T(1024)S(1)} %div.50), kind=kOutput, calls=%fused_computation.35 | convolution fusion | flops 3237492736 | bytes 11587600 | tf_op jit(solution)/shard_map/dot_general | solution.py:91
  96.7 8.7 %reshape.234 = bf16[2,257,3,16,64]{4,3,2,1,0:T(8,128)(2,1)} reshape(bf16[514,3072]{1,0:T(8,128)(2,1)} %fusion.20) | data formatting | bytes 6316032 | tf_op jit(solution)/shard_map/reshape | solution.py:58
  105.4 6.1 %fusion.107 = (bf16[2,257,1,16,64]{4,3,2,1,0:T(8,128)(2,1)S(1)}, bf16[2,257,1,16,64]{4,3,2,1,0:T(8,128)(2,1)}, bf16[2,257,1,16,64]{4,3,2,1,0:T(8,128)(2,1)}) fusion(bf16[2,257,3,16,64]{4,3,2,1,0:T(8,128)(2,1)} %reshape.234), kind=kLoop, calls=%fused_computation.139 | loop fusion | bytes 6316032 | tf_op jit(solution)/shard_map/slice | solution.py:63
  111.4 4.3 %copy.72 = bf16[2,257,1,16,64]{1,4,3,0,2:T(8,128)(2,1)} copy(bf16[2,257,1,16,64]{4,3,2,1,0:T(8,128)(2,1)} %get-tuple-element.5) | data formatting | bytes 2105344
  115.7 4.3 %copy.73 = bf16[2,257,1,16,64]{1,4,3,0,2:T(8,128)(2,1)} copy(bf16[2,257,1,16,64]{4,3,2,1,0:T(8,128)(2,1)} %get-tuple-element.6) | data formatting | bytes 2105344
  120.0 4.1 %copy.71 = bf16[2,257,1,16,64]{1,4,3,0,2:T(8,128)(2,1)} copy(bf16[2,257,1,16,64]{4,3,2,1,0:T(8,128)(2,1)S(1)} %get-tuple-element.4) | data formatting | bytes 2105344
  124.2 9.4 %fusion.41 = f32[2,16,257,257]{2,3,1,0:T(8,128)} fusion(bf16[2,257,1,16,64]{1,4,3,0,2:T(8,128)(2,1)} %copy.73, bf16[2,257,1,16,64]{1,4,3,0,2:T(8,128)(2,1)} %copy.72), kind=kOutput, calls=%fused_computation.55 | convolution fusion | flops 270536704 | bytes 10559616 | tf_op jit(solution)/shard_map/bqhd,bkhd->bhqk/dot_general | solution.py:59
  133.5 17.2 %fusion.108 = (f32[2,16,257]{2,1,0:T(8,128)S(1)}, f32[2,16,257,257]{2,3,1,0:T(8,128)}) fusion(f32[2,16,257,257]{2,3,1,0:T(8,128)} %fusion.41), kind=kOutput, calls=%fused_computation.140 | output fusion | flops 8454528 | bytes 16941440 | tf_op jit(solution)/shard_map/sub | solution.py:62
  150.7 6.4 %fusion.45 = bf16[2,257,16,64]{1,3,2,0:T(8,128)(2,1)S(1)} fusion(f32[2,16,257,257]{2,3,1,0:T(8,128)} %get-tuple-element.10, f32[2,16,257]{2,1,0:T(8,128)S(1)} %get-tuple-element.9, bf16[2,257,1,16,64]{1,4,3,0,2:T(8,128)(2,1)S(1)} %copy-done.2), kind=kOutput, calls=%fused_computation.59 | convolution fusion | flops 275290176 | bytes 10592512 | tf_op jit(solution)/shard_map/bhqk,bkhd->bqhd/dot_general | solution.py:63
  160.0 3.7 %convert_reduce_fusion = (f32[514]{0:T(1024)S(1)}, bf16[514,1024]{1,0:T(8,128)(2,1)S(1)}) fusion(f32[514,1024]{1,0:T(8,128)} %reshape.190, bf16[514,1024]{0,1:T(8,128)(2,1)S(1)} %reshape.184, bf16[1024,8192]{1,0:T(8,128)(2,1)} %all-gather.4.cloned.1.call-done), kind=kOutput, calls=%fused_computation.39 | convolution fusion | flops 1080040960 | bytes 6334472 | tf_op jit(solution)/shard_map/dot_general | solution.py:93
  164.1 26.2 %fusion.40.clone.4 = bf16[514,4096]{1,0:T(8,128)(2,1)} fusion(bf16[1024,8192]{1,0:T(8,128)(2,1)} %all-gather.4.cloned.1.call-done, bf16[514,1024]{1,0:T(8,128)(2,1)S(1)} %get-tuple-element.12, f32[1024]{0:T(1024)S(1)} %copy-done.6, f32[514]{0:T(1024)S(1)} %add_rsqrt_fusion.2, f32[514]{0:T(1024)S(1)} %broadcast_multiply_fusion.2), kind=kOutput, calls=%fused_computation.13.clone.clone.clone.clone.clone.clone.1 | convolution fusion | flops 4451223552 | bytes 13660176 | tf_op jit(solution)/shard_map/dot_general | solution.py:96
  190.3 8.7 %fusion.109 = (f32[514]{0:T(1024)S(1)}, f32[514,1024]{1,0:T(8,128)S(1)}) fusion(bf16[4096,1024]{1,0:T(8,128)(2,1)} %all-gather.6.cloned.1.call-done, bf16[514,1024]{1,0:T(8,128)(2,1)S(1)} %get-tuple-element.12, bf16[514,4096]{1,0:T(8,128)(2,1)} %fusion.40.clone.4), kind=kOutput, calls=%fused_computation.141 | convolution fusion | flops 4313323008 | bytes 15759368 | tf_op jit(solution)/shard_map/dot_general | solution.py:98
  204.8 4.0 %all_to_all.41 = f32[64,2,1,2,256]{4,3,0,2,1:T(2,128)S(1)} all-to-all(f32[64,2,1,2,256]{4,3,0,2,1:T(2,128)S(1)} %copy.62), channel_id=1, replica_groups=mesh['grp'=4,'fsdp_0'=4,'fsdp_1'=4,'fsdp_2'=2] {'fsdp_2'}, dimensions={1} | all-to-all | bytes 524288 | tf_op jit(solution)/shard_map/all_to_all | solution.py:39
  209.5 8.1 %all-to-all-start.3 = ((f32[64,2,1,2,256]{4,3,1,2,0:T(2,128)}), f32[64,2,1,2,256]{4,3,1,2,0:T(2,128)S(1)}, u32[]{:S(2)}, u32[]{:S(2)}) async-start(f32[64,2,1,2,256]{4,3,1,2,0:T(2,128)} %copy.63), calls=%async_computation.3 | async-start | bytes 524288 | tf_op jit(solution)/shard_map/all_to_all | solution.py:39
  221.2 6.4 %all-to-all-done.3 = f32[64,2,1,2,256]{4,3,1,2,0:T(2,128)S(1)} async-done(((f32[64,2,1,2,256]{4,3,1,2,0:T(2,128)}), f32[64,2,1,2,256]{4,3,1,2,0:T(2,128)S(1)}, u32[]{:S(2)}, u32[]{:S(2)}) %all-to-all-start.3) | async-done | bytes 262176 | tf_op jit(solution)/shard_map/all_to_all | solution.py:39
  228.5 5.1 %all-to-all-start.4 = ((f32[128,2,256]{2,1,0:T(2,128)}), f32[128,2,256]{2,1,0:T(2,128)S(1)}, u32[]{:S(2)}, u32[]{:S(2)}) async-start(f32[128,2,256]{2,1,0:T(2,128)} %fusion.65), calls=%async_computation.4 | async-start | bytes 524288 | tf_op jit(solution)/shard_map/all_to_all | solution.py:141
  234.5 3.9 %scatter_custom_fusion.2 = f32[2048,256]{1,0:T(8,128)} fusion(s32[256]{0:T(256)S(1)} %bitcast.73, f32[]{:T(128)} %constant.41.clone.1, f32[256,256]{1,0:T(8,128)S(1)} %gather_fusion, f32[256,256]{1,0:T(8,128)} %reshape_reshape_reshape.17, pred[256]{0:T(512)(128)(4,1)S(1)} %ge.24), kind=kCustom, calls=%fused_computation.67 | custom fusion | flops 196608 | bytes 2622976 | tf_op jit(solution)/shard_map/scatter-add | solution.py:140
  238.3 4.7 %fusion.63 = (f32[1,2048,256]{2,1,0:T(8,128)}, f32[1,2048,256]{2,1,0:T(8,128)}) fusion(f32[2048,256]{1,0:T(8,128)} %scatter_custom_fusion.2, f32[1,2048,256]{2,1,0:T(8,128)} %param.24, f32[1,2048,256]{2,1,0:T(8,128)S(1)} %copy-done.1), kind=kLoop, calls=%fused_computation.69 | loop fusion | flops 2621440 | bytes 10485760 | tf_op jit(solution)/shard_map/broadcast_in_dim | solution.py:166
  244.6 8.3 %all-to-all-start.5 = ((bf16[2,128,8]{2,0,1:T(2,128)(2,1)}), bf16[2,128,8]{2,0,1:T(2,128)(2,1)S(1)}, u32[]{:S(2)}, u32[]{:S(2)}) async-start(bf16[2,128,8]{2,0,1:T(2,128)(2,1)} %copy.66), calls=%async_computation.5 | async-start | bytes 131072 | tf_op jit(solution)/shard_map/all_to_all | solution.py:156
  254.1 37.0 %all-gather = f32[128,2,256]{2,1,0:T(2,128)S(1)} all-gather(f32[1,2,256]{2,1,0:T(2,128)S(1)} %bitcast.69), channel_id=1, replica_groups=mesh['grp'=4,'fsdp_0'=4,'fsdp_1'=4,'fsdp_2'=2] {'grp','fsdp_0','fsdp_1',..., dimensions={0}, use_global_device_ids=true | all-gather | bytes 264192 | tf_op jit(solution)/shard_map/all_gather | solution.py:155
  (86 shorter events, 32.8 us)
Async XLA Ops:
  7.2 195.9 %copy-start = (bf16[1024,256]{1,0:T(8,128)(2,1)S(1)}, bf16[1024,256]{1,0:T(8,128)(2,1)}, u32[]{:S(2)}) copy-start(bf16[1024,256]{1,0:T(8,128)(2,1)} %param.22) | copy-start | bytes 1572868
  7.2 80.7 %all-gather.4.cloned.1.call-start = ((), (), s32[]{:S(2)}) async-start(), calls=%async_computation.6 | async-start | bytes 17301504 | tf_op jit(solution)/shard_map/all_gather | solution.py:19
  9.1 78.7 %copy-start.5 = (f32[1024]{0:T(1024)S(1)}, f32[1024]{0:T(1024)}, u32[]{:S(2)}) copy-start(f32[1024]{0:T(1024)} %param.15) | copy-start | bytes 12292
  9.2 181.1 %all-gather.6.cloned.1.call-start = ((), (), s32[]{:S(2)}) async-start(), calls=%async_computation.7 | async-start | bytes 8650752 | tf_op jit(solution)/shard_map/all_gather | solution.py:88
  19.4 20.5 %all-to-all-start.1 = ((s32[64,2,1,2]{3,1,2,0:T(2,128)}), s32[64,2,1,2]{3,1,2,0:T(2,128)S(1)}, u32[]{:S(2)}, u32[]{:S(2)}) async-start(s32[64,2,1,2]{3,1,2,0:T(2,128)} %copy.51), calls=%async_computation.1 | async-start | bytes 131072 | tf_op jit(solution)/shard_map/all_to_all | solution.py:39
  133.5 17.2 %copy-start.2 = (bf16[2,257,1,16,64]{1,4,3,0,2:T(8,128)(2,1)S(1)}, bf16[2,257,1,16,64]{1,4,3,0,2:T(8,128)(2,1)}, u32[]{:S(2)}) copy-start(bf16[2,257,1,16,64]{1,4,3,0,2:T(8,128)(2,1)} %copy.71) | copy-start | bytes 3158020
  160.0 4.1 %copy-start.6 = (f32[1024]{0:T(1024)S(1)}, f32[1024]{0:T(1024)}, u32[]{:S(2)}) copy-start(f32[1024]{0:T(1024)} %param.18) | copy-start | bytes 12292
  190.3 9.1 %copy-start.4 = (f32[1024]{0:T(1024)S(1)}, f32[1024]{0:T(1024)}, u32[]{:S(2)}) copy-start(f32[1024]{0:T(1024)} %param.21) | copy-start | bytes 12292
  203.0 35.3 %copy-start.1 = (f32[1,2048,256]{2,1,0:T(8,128)S(1)}, f32[1,2048,256]{2,1,0:T(8,128)}, u32[]{:S(2)}) copy-start(f32[1,2048,256]{2,1,0:T(8,128)} %param.23) | copy-start | bytes 6291460
  209.5 18.0 %all-to-all-start.3 = ((f32[64,2,1,2,256]{4,3,1,2,0:T(2,128)}), f32[64,2,1,2,256]{4,3,1,2,0:T(2,128)S(1)}, u32[]{:S(2)}, u32[]{:S(2)}) async-start(f32[64,2,1,2,256]{4,3,1,2,0:T(2,128)} %copy.63), calls=%async_computation.3 | async-start | bytes 524288 | tf_op jit(solution)/shard_map/all_to_all | solution.py:39
  228.5 16.0 %all-to-all-start.4 = ((f32[128,2,256]{2,1,0:T(2,128)}), f32[128,2,256]{2,1,0:T(2,128)S(1)}, u32[]{:S(2)}, u32[]{:S(2)}) async-start(f32[128,2,256]{2,1,0:T(2,128)} %fusion.65), calls=%async_computation.4 | async-start | bytes 524288 | tf_op jit(solution)/shard_map/all_to_all | solution.py:141
  244.6 46.8 %all-to-all-start.5 = ((bf16[2,128,8]{2,0,1:T(2,128)(2,1)}), bf16[2,128,8]{2,0,1:T(2,128)(2,1)S(1)}, u32[]{:S(2)}, u32[]{:S(2)}) async-start(bf16[2,128,8]{2,0,1:T(2,128)(2,1)} %copy.66), calls=%async_computation.5 | async-start | bytes 131072 | tf_op jit(solution)/shard_map/all_to_all | solution.py:156
  254.1 38.0 %copy-start.3 = (f32[2,256]{1,0:T(2,128)}, f32[2,256]{1,0:T(2,128)S(1)}, u32[]{:S(2)}) copy-start(f32[2,256]{1,0:T(2,128)S(1)} %subtract_multiply_fusion) | copy-start | bytes 6148
Sparse Core Ops, SparseCore 0:
  10.8 77.0 all-gather.3
  90.1 52.2 all-gather.5
where the time goes:
time: 303 us; the launch traced here: 299 us
  matrix products  64.2 us (21%)
  waiting for transfers between devices  56.6 us (19%)
  local copies, waits for them, and re-layouts  46.3 us (15%)
  blocking collectives  45.8 us (15%)
  other arithmetic  38.7 us (13%)
  starting transfers between devices  33.1 us (11%)
  between operations  14.6 us (5%)
    all_gather x1, waiting for transfers between devices, sent_together(): out = lax.all_gather(both, axis, axis=dim, tiled=True)  47.6 us
    all_gather x1, blocking collectives, on_device(): every_grad = lax.all_gather(content_grad, GRP_FSDP, axis=0, tiled=True)  37 us
    dot_general x1, matrix products, on_device(): upward = jnp.dot(normed_two, full_up, preferred_element_type=jnp.float32)  26.2 us
    all_to_all x2, starting transfers between devices, turned_blocks(): lax.all_to_all(tiles, axes[k], split_axis=k, concat_axis=k, tiled=True)  19.6 us
    sub x1, other arithmetic, attend(): probs = jax.nn.softmax(scores, axis=-1).astype(jnp.bfloat16)  17.2 us
    unnamed x22, local copies, waits for them, and re-layouts  13.3 us
    dot_general x1, matrix products, attend(): jnp.einsum('bqhd,bkhd->bhqk', parts[:, :, 0], parts[:, :, 1], preferred_e...  9.35 us
    dot_general x1, matrix products, on_device(): qkv = jnp.dot(normed, full_qkv, preferred_element_type=jnp.float32)  8.78 us
  transfers between devices with their start and end apart: 6, of which 4 were waited for; matrix products, arithmetic and copies ran while one was open for 44% of the time, Pallas kernels for 0%

commit v1 on v0

--- a/solution.py
+++ b/solution.py
@@ -152,7 +152,16 @@
     inner = jnp.mean(grad_unit * unit, axis=-1, keepdims=True)
     content_grad = scale * (grad_unit - unit * inner)
     share = width // n_devices
-    every_grad = lax.all_gather(content_grad, GRP_FSDP, axis=0, tiled=True)
+    define_the_halves = lambda my_data, d0: jnp.concatenate(
+        lax.all_to_all(
+            jnp.stack(lax.axis_size(GRP_FSDP) * [my_data]),
+            axis_name=GRP_FSDP,
+            split_axis=0,
+            concat_axis=0,
+        ),
+        d0,
+    )
+    every_grad = define_the_halves(content_grad, 0)
     my_columns = lax.all_to_all(
         pooled.reshape(images, n_devices, share), GRP_FSDP, split_axis=1, concat_axis=0, tiled=True
     )

time: 303 us -> 290 us (0.957)
  blocking collectives: 45.8 us -> 8.88 us
  waiting for transfers between devices: 56.6 us -> 75.8 us
    all_gather x1 -> x0, blocking collectives: 37 us -> none  [on_device(): every_grad = lax.all_gather(content_grad, GRP_FSDP, axis=0, tiled=True)]
    all_to_all x1, waiting for transfers between devices: 1.5 us -> 10.7 us  [on_device(): lax.all_to_all(-diff.reshape(n_devices, slots, proj_width), GRP_FSDP, spl...]
    all_to_all x0 -> x1, waiting for transfers between devices: none -> 4.56 us  [on_device(): lax.all_to_all(jnp.stack(lax.axis_size(GRP_FSDP) * [my_data]), axis_name=...]
    all_to_all x1, waiting for transfers between devices: 0.01 us -> 4.52 us  [on_device(): lax.all_to_all(pooled.reshape(images, n_devices, share), GRP_FSDP, split_...]
    all_to_all x0 -> x1, starting transfers between devices: none -> 4.44 us  [on_device(): lax.all_to_all(jnp.stack(lax.axis_size(GRP_FSDP) * [my_data]), axis_name=...]
    unnamed x22 -> x25, local copies, waits for them, and re-layouts: 13.3 us -> 13.2 us
  transfers between devices with their start and end apart: 6 -> 7, of which waited for: 4 -> 6; matrix products, arithmetic and copies ran while one was open for 44% -> 45% of each run, Pallas kernels for 0% -> 0%
where the time goes in v1:
time: 290 us; the launch traced here: 287 us
  waiting for transfers between devices  75.8 us (26%)
  matrix products  64.2 us (22%)
  local copies, waits for them, and re-layouts  48.8 us (17%)
  other arithmetic  38.7 us (13%)
  starting transfers between devices  35.5 us (12%)
  between operations  14.6 us (5%)
  blocking collectives  8.88 us (3%)
    all_gather x1, waiting for transfers between devices, sent_together(): out = lax.all_gather(both, axis, axis=dim, tiled=True)  47.8 us
    dot_general x1, matrix products, on_device(): upward = jnp.dot(normed_two, full_up, preferred_element_type=jnp.float32)  26.2 us
    all_to_all x2, starting transfers between devices, turned_blocks(): lax.all_to_all(tiles, axes[k], split_axis=k, concat_axis=k, tiled=True)  19.6 us
    sub x1, other arithmetic, attend(): probs = jax.nn.softmax(scores, axis=-1).astype(jnp.bfloat16)  17.2 us
    unnamed x25, local copies, waits for them, and re-layouts  13.2 us
    all_to_all x1, waiting for transfers between devices, on_device(): lax.all_to_all(-diff.reshape(n_devices, slots, proj_width), GRP_FSDP, spl...  10.7 us
    dot_general x1, matrix products, attend(): jnp.einsum('bqhd,bkhd->bhqk', parts[:, :, 0], parts[:, :, 1], preferred_e...  9.35 us
    all_to_all x2, blocking collectives, turned_blocks(): lax.all_to_all(tiles, axes[k], split_axis=k, concat_axis=k, tiled=True)  8.88 us
  transfers between devices with their start and end apart: 7, of which 6 were waited for; matrix products, arithmetic and copies ran while one was open for 45% of the time, Pallas kernels for 0%

profile of v1, /device:TPU:1, one launch (start us, length us, event | category | flops | bytes accessed | tf_op | source)
XLA Modules:
  0.0 286.5 jit_solution(7880709803776496600)
XLA Ops:
  12.7 4.7 %all_to_all.45 = s32[2,1,128]{2,1,0:T(1,128)S(1)} all-to-all(s32[2,1,128]{2,1,0:T(1,128)S(1)} %reshape.245), channel_id=1, replica_groups=mesh['grp'=4,'fsdp_0'=4,'fsdp_1'=4,'fsdp_2'=2] {'fsdp_2'}, dimensions={0} | all-to-all | bytes 2048 | tf_op jit(solution)/shard_map/all_to_all | solution.py:39
  19.4 11.5 %all-to-all-start.1 = ((s32[64,2,1,2]{3,1,2,0:T(2,128)}), s32[64,2,1,2]{3,1,2,0:T(2,128)S(1)}, u32[]{:S(2)}, u32[]{:S(2)}) async-start(s32[64,2,1,2]{3,1,2,0:T(2,128)} %copy.51), calls=%async_computation.1 | async-start | bytes 131072 | tf_op jit(solution)/shard_map/all_to_all | solution.py:39
  40.1 47.8 %all-gather.3.cloned.1.call-done = bf16[1024,8192]{1,0:T(8,128)(2,1)} async-done(((bf16[32,8192]{1,0:T(8,128)(2,1)}), bf16[1024,8192]{1,0:T(8,128)(2,1)}) %all-gather.3.cloned.1.call-update) | async-done | bytes 16777232 | tf_op jit(solution)/shard_map/all_gather | solution.py:19
  87.9 8.8 %fusion.20 = bf16[514,3072]{1,0:T(8,128)(2,1)} fusion(bf16[1024,8192]{1,0:T(8,128)(2,1)} %all-gather.3.cloned.1.call-done, f32[514,1024]{1,0:T(8,128)} %reshape.196, f32[1024]{0:T(1024)S(1)} %copy-done.7, f32[514]{0:T(1024)S(1)} %rsqrt.37, f32[514]{0:T(1024)S(1)} %div.50), kind=kOutput, calls=%fused_computation.35 | convolution fusion | flops 3237492736 | bytes 11587600 | tf_op jit(solution)/shard_map/dot_general | solution.py:91
  96.7 8.7 %reshape.238 = bf16[2,257,3,16,64]{4,3,2,1,0:T(8,128)(2,1)} reshape(bf16[514,3072]{1,0:T(8,128)(2,1)} %fusion.20) | data formatting | bytes 6316032 | tf_op jit(solution)/shard_map/reshape | solution.py:58
  105.4 6.1 %fusion.107 = (bf16[2,257,1,16,64]{4,3,2,1,0:T(8,128)(2,1)S(1)}, bf16[2,257,1,16,64]{4,3,2,1,0:T(8,128)(2,1)}, bf16[2,257,1,16,64]{4,3,2,1,0:T(8,128)(2,1)}) fusion(bf16[2,257,3,16,64]{4,3,2,1,0:T(8,128)(2,1)} %reshape.238), kind=kLoop, calls=%fused_computation.139 | loop fusion | bytes 6316032 | tf_op jit(solution)/shard_map/slice | solution.py:63
  111.4 4.3 %copy.72 = bf16[2,257,1,16,64]{1,4,3,0,2:T(8,128)(2,1)} copy(bf16[2,257,1,16,64]{4,3,2,1,0:T(8,128)(2,1)} %get-tuple-element.5) | data formatting | bytes 2105344
  115.7 4.3 %copy.73 = bf16[2,257,1,16,64]{1,4,3,0,2:T(8,128)(2,1)} copy(bf16[2,257,1,16,64]{4,3,2,1,0:T(8,128)(2,1)} %get-tuple-element.6) | data formatting | bytes 2105344
  120.0 4.1 %copy.71 = bf16[2,257,1,16,64]{1,4,3,0,2:T(8,128)(2,1)} copy(bf16[2,257,1,16,64]{4,3,2,1,0:T(8,128)(2,1)S(1)} %get-tuple-element.4) | data formatting | bytes 2105344
  124.2 9.4 %fusion.41 = f32[2,16,257,257]{2,3,1,0:T(8,128)} fusion(bf16[2,257,1,16,64]{1,4,3,0,2:T(8,128)(2,1)} %copy.73, bf16[2,257,1,16,64]{1,4,3,0,2:T(8,128)(2,1)} %copy.72), kind=kOutput, calls=%fused_computation.55 | convolution fusion | flops 270536704 | bytes 10559616 | tf_op jit(solution)/shard_map/bqhd,bkhd->bhqk/dot_general | solution.py:59
  133.5 17.2 %fusion.108 = (f32[2,16,257]{2,1,0:T(8,128)S(1)}, f32[2,16,257,257]{2,3,1,0:T(8,128)}) fusion(f32[2,16,257,257]{2,3,1,0:T(8,128)} %fusion.41), kind=kOutput, calls=%fused_computation.140 | output fusion | flops 8454528 | bytes 16941440 | tf_op jit(solution)/shard_map/sub | solution.py:62
  150.7 6.4 %fusion.45 = bf16[2,257,16,64]{1,3,2,0:T(8,128)(2,1)S(1)} fusion(f32[2,16,257,257]{2,3,1,0:T(8,128)} %get-tuple-element.10, f32[2,16,257]{2,1,0:T(8,128)S(1)} %get-tuple-element.9, bf16[2,257,1,16,64]{1,4,3,0,2:T(8,128)(2,1)S(1)} %copy-done.2), kind=kOutput, calls=%fused_computation.59 | convolution fusion | flops 275290176 | bytes 10592512 | tf_op jit(solution)/shard_map/bhqk,bkhd->bqhd/dot_general | solution.py:63
  164.1 26.2 %fusion.40.clone.4 = bf16[514,4096]{1,0:T(8,128)(2,1)} fusion(bf16[1024,8192]{1,0:T(8,128)(2,1)} %all-gather.3.cloned.1.call-done, bf16[514,1024]{1,0:T(8,128)(2,1)S(1)} %get-tuple-element.12, f32[1024]{0:T(1024)S(1)} %copy-done.8, f32[514]{0:T(1024)S(1)} %add_rsqrt_fusion.2, f32[514]{0:T(1024)S(1)} %broadcast_multiply_fusion.2), kind=kOutput, calls=%fused_computation.13.clone.clone.clone.clone.clone.clone.1 | convolution fusion | flops 4451223552 | bytes 13660176 | tf_op jit(solution)/shard_map/dot_general | solution.py:96
  190.3 8.7 %fusion.109 = (f32[514]{0:T(1024)S(1)}, f32[514,1024]{1,0:T(8,128)S(1)}) fusion(bf16[4096,1024]{1,0:T(8,128)(2,1)} %all-gather.5.cloned.1.call-done, bf16[514,1024]{1,0:T(8,128)(2,1)S(1)} %get-tuple-element.12, bf16[514,4096]{1,0:T(8,128)(2,1)} %fusion.40.clone.4), kind=kOutput, calls=%fused_computation.141 | convolution fusion | flops 4313323008 | bytes 15759368 | tf_op jit(solution)/shard_map/dot_general | solution.py:98
  204.8 4.1 %all_to_all.46 = f32[64,2,1,2,256]{4,3,0,2,1:T(2,128)S(1)} all-to-all(f32[64,2,1,2,256]{4,3,0,2,1:T(2,128)S(1)} %copy.62), channel_id=1, replica_groups=mesh['grp'=4,'fsdp_0'=4,'fsdp_1'=4,'fsdp_2'=2] {'fsdp_2'}, dimensions={1} | all-to-all | bytes 524288 | tf_op jit(solution)/shard_map/all_to_all | solution.py:39
  209.7 8.1 %all-to-all-start.3 = ((f32[64,2,1,2,256]{4,3,1,2,0:T(2,128)}), f32[64,2,1,2,256]{4,3,1,2,0:T(2,128)S(1)}, u32[]{:S(2)}, u32[]{:S(2)}) async-start(f32[64,2,1,2,256]{4,3,1,2,0:T(2,128)} %copy.63), calls=%async_computation.3 | async-start | bytes 524288 | tf_op jit(solution)/shard_map/all_to_all | solution.py:39
  220.6 7.1 %all-to-all-done.3 = f32[64,2,1,2,256]{4,3,1,2,0:T(2,128)S(1)} async-done(((f32[64,2,1,2,256]{4,3,1,2,0:T(2,128)}), f32[64,2,1,2,256]{4,3,1,2,0:T(2,128)S(1)}, u32[]{:S(2)}, u32[]{:S(2)}) %all-to-all-start.3) | async-done | bytes 262176 | tf_op jit(solution)/shard_map/all_to_all | solution.py:39
  228.7 6.1 %all-to-all-start.4 = ((f32[128,2,256]{2,1,0:T(2,128)}), f32[128,2,256]{2,1,0:T(2,128)}, u32[]{:S(2)}, u32[]{:S(2)}) async-start(f32[128,2,256]{2,1,0:T(2,128)} %fusion.65), calls=%async_computation.4 | async-start | bytes 524288 | tf_op jit(solution)/shard_map/all_to_all | solution.py:141
  234.7 10.7 %all-to-all-done.4 = f32[128,2,256]{2,1,0:T(2,128)} async-done(((f32[128,2,256]{2,1,0:T(2,128)}), f32[128,2,256]{2,1,0:T(2,128)}, u32[]{:S(2)}, u32[]{:S(2)}) %all-to-all-start.4) | async-done | bytes 262176 | tf_op jit(solution)/shard_map/all_to_all | solution.py:141
  248.4 4.4 %all-to-all-start.6 = ((f32[128,2,256]{2,1,0:T(2,128)}), f32[128,2,256]{2,1,0:T(2,128)S(1)}, u32[]{:S(2)}, u32[]{:S(2)}) async-start(f32[128,2,256]{2,1,0:T(2,128)} %stack.2), calls=%async_computation.6 | async-start | bytes 524288 | tf_op jit(solution)/shard_map/all_to_all | solution.py:156
  259.3 4.6 %all-to-all-done.6 = f32[128,2,256]{2,1,0:T(2,128)S(1)} async-done(((f32[128,2,256]{2,1,0:T(2,128)}), f32[128,2,256]{2,1,0:T(2,128)S(1)}, u32[]{:S(2)}, u32[]{:S(2)}) %all-to-all-start.6) | async-done | bytes 262176 | tf_op jit(solution)/shard_map/all_to_all | solution.py:156
  263.9 5.3 %all-to-all-start.5 = ((bf16[2,128,8]{2,0,1:T(2,128)(2,1)}), bf16[2,128,8]{2,0,1:T(2,128)(2,1)S(1)}, u32[]{:S(2)}, u32[]{:S(2)}) async-start(bf16[2,128,8]{2,0,1:T(2,128)(2,1)} %copy.66), calls=%async_computation.5 | async-start | bytes 131072 | tf_op jit(solution)/shard_map/all_to_all | solution.py:165
  269.2 4.7 %fusion.63 = (f32[1,2048,256]{2,1,0:T(8,128)}, f32[1,2048,256]{2,1,0:T(8,128)}) fusion(f32[2048,256]{1,0:T(8,128)} %scatter_custom_fusion.2, f32[1,2048,256]{2,1,0:T(8,128)} %param.24, f32[1,2048,256]{2,1,0:T(8,128)S(1)} %copy-done.1), kind=kLoop, calls=%fused_computation.69 | loop fusion | flops 2621440 | bytes 10485760 | tf_op jit(solution)/shard_map/broadcast_in_dim | solution.py:175
  274.1 4.5 %all-to-all-done.5 = bf16[2,128,8]{2,0,1:T(2,128)(2,1)S(1)} async-done(((bf16[2,128,8]{2,0,1:T(2,128)(2,1)}), bf16[2,128,8]{2,0,1:T(2,128)(2,1)S(1)}, u32[]{:S(2)}, u32[]{:S(2)}) %all-to-all-start.5) | async-done | bytes 4128 | tf_op jit(solution)/shard_map/all_to_all | solution.py:165
  (92 shorter events, 44.1 us)
Async XLA Ops:
  7.2 195.9 %copy-start = (bf16[1024,256]{1,0:T(8,128)(2,1)S(1)}, bf16[1024,256]{1,0:T(8,128)(2,1)}, u32[]{:S(2)}) copy-start(bf16[1024,256]{1,0:T(8,128)(2,1)} %param.22) | copy-start | bytes 1572868
  7.2 80.7 %all-gather.3.cloned.1.call-start = ((), (), s32[]{:S(2)}) async-start(), calls=%async_computation.7 | async-start | bytes 17301504 | tf_op jit(solution)/shard_map/all_gather | solution.py:19
  9.1 78.7 %copy-start.7 = (f32[1024]{0:T(1024)S(1)}, f32[1024]{0:T(1024)}, u32[]{:S(2)}) copy-start(f32[1024]{0:T(1024)} %param.15) | copy-start | bytes 12292
  9.2 181.1 %all-gather.5.cloned.1.call-start = ((), (), s32[]{:S(2)}) async-start(), calls=%async_computation.8 | async-start | bytes 8650752 | tf_op jit(solution)/shard_map/all_gather | solution.py:88
  19.4 20.5 %all-to-all-start.1 = ((s32[64,2,1,2]{3,1,2,0:T(2,128)}), s32[64,2,1,2]{3,1,2,0:T(2,128)S(1)}, u32[]{:S(2)}, u32[]{:S(2)}) async-start(s32[64,2,1,2]{3,1,2,0:T(2,128)} %copy.51), calls=%async_computation.1 | async-start | bytes 131072 | tf_op jit(solution)/shard_map/all_to_all | solution.py:39
  40.1 177.7 %copy-start.6 = (s32[256,1]{0,1:T(1,128)}, s32[256,1]{0,1:T(1,128)S(1)}, u32[]{:S(2)}) copy-start(s32[256,1]{0,1:T(1,128)S(1)} %compare_select_fusion) | copy-start | bytes 3076
  133.5 17.2 %copy-start.2 = (bf16[2,257,1,16,64]{1,4,3,0,2:T(8,128)(2,1)S(1)}, bf16[2,257,1,16,64]{1,4,3,0,2:T(8,128)(2,1)}, u32[]{:S(2)}) copy-start(bf16[2,257,1,16,64]{1,4,3,0,2:T(8,128)(2,1)} %copy.71) | copy-start | bytes 3158020
  160.0 4.1 %copy-start.8 = (f32[1024]{0:T(1024)S(1)}, f32[1024]{0:T(1024)}, u32[]{:S(2)}) copy-start(f32[1024]{0:T(1024)} %param.18) | copy-start | bytes 12292
  190.3 9.1 %copy-start.5 = (f32[1024]{0:T(1024)S(1)}, f32[1024]{0:T(1024)}, u32[]{:S(2)}) copy-start(f32[1024]{0:T(1024)} %param.21) | copy-start | bytes 12292
  204.7 64.5 %copy-start.1 = (f32[1,2048,256]{2,1,0:T(8,128)S(1)}, f32[1,2048,256]{2,1,0:T(8,128)}, u32[]{:S(2)}) copy-start(f32[1,2048,256]{2,1,0:T(8,128)} %param.23) | copy-start | bytes 6291460
  209.7 18.0 %all-to-all-start.3 = ((f32[64,2,1,2,256]{4,3,1,2,0:T(2,128)}), f32[64,2,1,2,256]{4,3,1,2,0:T(2,128)S(1)}, u32[]{:S(2)}, u32[]{:S(2)}) async-start(f32[64,2,1,2,256]{4,3,1,2,0:T(2,128)} %copy.63), calls=%async_computation.3 | async-start | bytes 524288 | tf_op jit(solution)/shard_map/all_to_all | solution.py:39
  220.6 24.9 %copy-start.3 = (pred[64,2,1,2]{3,1,2,0:T(4,128)(4,1)}, pred[64,2,1,2]{3,1,2,0:T(4,128)(4,1)S(1)}, u32[]{:S(2)}) copy-start(pred[64,2,1,2]{3,1,2,0:T(4,128)(4,1)S(1)} %broadcast_compare_fusion) | copy-start | bytes 772
  228.7 16.8 %all-to-all-start.4 = ((f32[128,2,256]{2,1,0:T(2,128)}), f32[128,2,256]{2,1,0:T(2,128)}, u32[]{:S(2)}, u32[]{:S(2)}) async-start(f32[128,2,256]{2,1,0:T(2,128)} %fusion.65), calls=%async_computation.4 | async-start | bytes 524288 | tf_op jit(solution)/shard_map/all_to_all | solution.py:141
  247.6 26.3 %copy-start.4 = (f32[2,256]{1,0:T(2,128)}, f32[2,256]{1,0:T(2,128)S(1)}, u32[]{:S(2)}) copy-start(f32[2,256]{1,0:T(2,128)S(1)} %subtract_multiply_fusion) | copy-start | bytes 6148
  248.4 15.5 %all-to-all-start.6 = ((f32[128,2,256]{2,1,0:T(2,128)}), f32[128,2,256]{2,1,0:T(2,128)S(1)}, u32[]{:S(2)}, u32[]{:S(2)}) async-start(f32[128,2,256]{2,1,0:T(2,128)} %stack.2), calls=%async_computation.6 | async-start | bytes 524288 | tf_op jit(solution)/shard_map/all_to_all | solution.py:156
  263.9 14.8 %all-to-all-start.5 = ((bf16[2,128,8]{2,0,1:T(2,128)(2,1)}), bf16[2,128,8]{2,0,1:T(2,128)(2,1)S(1)}, u32[]{:S(2)}, u32[]{:S(2)}) async-start(bf16[2,128,8]{2,0,1:T(2,128)(2,1)} %copy.66), calls=%async_computation.5 | async-start | bytes 131072 | tf_op jit(solution)/shard_map/all_to_all | solution.py:165
Sparse Core Ops, SparseCore 0:
  10.8 77.0 all-gather.2
  90.1 52.2 all-gather.4
